TPU v7x, 32 devices: a whole 2x2x4 slice. The times are simulated.
32 devices in a mesh: dp: 2 (over x), row: 4 (over y, core), col: 4 (over z).
Axes of the slice: x: 2, y: 2, z: 4, core: 2. Of those that a mesh axis runs over, the one named last changes fastest.
Arguments:
- inputs: bfloat16 [14568, 12, 128], P(('dp', 'row'), 'col'), may hold values from -15 to 15
- mixer_weight: float32 [768, 2304], P('row', 'col'), may hold values from -0.3125 to 0.3125
- mixer_bias: float32 [12, 128], P('col', 'row'), may hold values from -3 to 3
- merge_weight: float32 [768, 768], P(('col', 'row')), may hold values from -0.875 to 0.875
- merge_bias: float32 [12, 64], P('col', 'row'), may hold values from -3 to 3
- expand_weight: float32 [768, 3072], P('row', 'col'), may hold values from -0.21875 to 0.21875
- expand_bias: float32 [12, 256], P('col', 'row'), may hold values from -3 to 3
- reduce_weight: float32 [3072, 768], P(('col', 'row')), may hold values from -0.109375 to 0.109375
- reduce_bias: float32 [12, 64], P('col', 'row'), may hold values from -3 to 3
- first_gain: float32 [12, 64], P('col', 'row'), may hold values from 0.1 to 1.9
- first_shift: float32 [12, 64], P('col', 'row'), may hold values from -3 to 3
- second_gain: float32 [12, 64], P('col', 'row'), may hold values from 0.1 to 1.9
- second_shift: float32 [12, 64], P('col', 'row'), may hold values from -3 to 3
- cotangent: bfloat16 [14568, 12, 128], P(('dp', 'row'), 'col'), may hold values from -6 to 6
Outputs:
- outputs: bfloat16 [14568, 12, 128], P(('dp', 'row'), 'col')
- input_grad: float32 [14568, 12, 128], P(('dp', 'row'), 'col')
- grad_mixer_weight: float32 [768, 2304], P('row', 'col')
- grad_mixer_bias: float32 [12, 128], P('col', 'row')
- grad_merge_weight: float32 [768, 768], P(('col', 'row'))
- grad_merge_bias: float32 [12, 64], P('col', 'row')
- grad_expand_weight: float32 [768, 3072], P('row', 'col')
- grad_expand_bias: float32 [12, 256], P('col', 'row')
- grad_reduce_weight: float32 [3072, 768], P(('col', 'row'))
- grad_reduce_bias: float32 [12, 64], P('col', 'row')
- grad_first_gain: float32 [12, 64], P('col', 'row')
- grad_first_shift: float32 [12, 64], P('col', 'row')
- grad_second_gain: float32 [12, 64], P('col', 'row')
- grad_second_shift: float32 [12, 64], P('col', 'row')
All inputs are finite; a program needn't handle non-finite values.
Results may differ from a plain program's by a relative error of at most 0.012.
The roundings to bfloat16 on the way count: a program that leaves them out, or rounds other values in their place, can miss the bound.
Values may be sent and summed in bfloat16 or wider, within the bound.
A program may use at most 192 MiB of HBM per device.

v0:
```python
import jax
import jax.numpy as jnp
from jax import lax
from jax.sharding import PartitionSpec as P

D = 768
HD = 64
LEN = 1214
EPSILON = 1e-06


def to_rows(values):
    halves = values.shape[0]
    groups = values.shape[1]
    return (
        values.reshape(halves, groups, 2, HD).transpose(0, 2, 1, 3).reshape(2 * halves, groups * HD)
    )


def from_rows(values):
    halves = values.shape[0] // 2
    groups = values.shape[1] // HD
    return (
        values.reshape(halves, 2, groups, HD).transpose(0, 2, 1, 3).reshape(halves, groups, 2 * HD)
    )


def exact_gelu(values):
    return jax.nn.gelu(values, approximate=False)


def inner_rows(left, right):
    return lax.dot_general(
        left, right, (((0,), (0,)), ((), ())), preferred_element_type=jnp.float32
    )


def times_transposed(left, right):
    return lax.dot_general(
        left, right, (((1,), (1,)), ((), ())), preferred_element_type=jnp.float32
    )


def as_vector(values):
    return values.astype(jnp.float32).reshape(-1)


def row_sum(values):
    return lax.psum(values, "col")


def norm_shard(values, gain, shift):
    centre = row_sum(jnp.sum(values, axis=1)) / D
    centered = values - centre[:, None]
    spread = row_sum(jnp.sum(centered * centered, axis=1)) / D
    inverse = lax.rsqrt(spread + EPSILON)
    scaled = centered * inverse[:, None]
    return (scaled * gain + shift, scaled, inverse)


def spread_rows(values):
    return lax.all_gather(values, "col", axis=1, tiled=True)


def gather_grads(values):
    return lax.all_gather(values, "col", axis=1, tiled=True)


def norm_back(partial_rows, scaled, inverse, gain):
    shard = lax.psum_scatter(partial_rows, "col", scatter_dimension=1, tiled=True)
    grad_gain = jnp.sum(shard * scaled, axis=0)
    grad_shift = jnp.sum(shard, axis=0)
    upstream = shard * gain
    first_sum, second_sum = lax.psum(
        (jnp.sum(upstream, axis=1), jnp.sum(upstream * scaled, axis=1)), "col"
    )
    result = inverse[:, None] * (
        upstream - first_sum[:, None] / D - scaled * (second_sum[:, None] / D)
    )
    return (result, grad_gain, grad_shift)


def attend(parts):
    query, keyset, valueset = parts
    scores = times_transposed(query, keyset) * HD ** (-0.5)
    highest = jnp.max(scores, axis=1, keepdims=True)
    weights = jnp.exp(scores - highest)
    totals = jnp.sum(weights, axis=1, keepdims=True)
    chances = (weights / totals).astype(jnp.bfloat16)
    result = jnp.dot(chances, valueset, preferred_element_type=jnp.float32)
    return (result.astype(jnp.bfloat16), (highest + jnp.log(totals))[:, 0])


def attend_back(parts):
    query, keyset, valueset, upstream, logsum = parts
    scale = HD ** (-0.5)
    scores = times_transposed(query, keyset) * scale
    chances = jnp.exp(scores - logsum[:, None])
    grad_chances = times_transposed(upstream, valueset)
    grad_value = inner_rows(chances.astype(jnp.bfloat16), upstream)
    inner = jnp.sum(grad_chances * chances, axis=1, keepdims=True)
    grad_scores = (chances * (grad_chances - inner)).astype(jnp.bfloat16)
    grad_query = jnp.dot(grad_scores, keyset, preferred_element_type=jnp.float32) * scale
    grad_key = inner_rows(grad_scores, query) * scale
    return jnp.stack([grad_query, grad_key, grad_value], axis=1).astype(jnp.bfloat16)


def body(
    inputs,
    mixer_weight,
    mixer_bias,
    merge_weight,
    merge_bias,
    expand_weight,
    expand_bias,
    reduce_weight,
    reduce_bias,
    first_gain,
    first_shift,
    second_gain,
    second_shift,
    cotangent,
):
    (
        mixer_mat,
        mixer_vec,
        merge_mat,
        merge_vec,
        expand_mat,
        expand_vec,
        reduce_mat,
        reduce_vec,
        gain_one,
        shift_one,
        gain_two,
        shift_two,
    ) = (
        lax.all_gather(mixer_weight.astype(jnp.bfloat16), "row", axis=0, tiled=True),
        lax.all_gather(mixer_bias.astype(jnp.bfloat16), "row", axis=1, tiled=True),
        lax.all_gather(merge_weight.astype(jnp.bfloat16), "row", axis=0, tiled=True),
        lax.all_gather(merge_bias.astype(jnp.bfloat16), "row", axis=1, tiled=True),
        lax.all_gather(expand_weight.astype(jnp.bfloat16), "row", axis=0, tiled=True),
        lax.all_gather(expand_bias.astype(jnp.bfloat16), "row", axis=1, tiled=True),
        lax.all_gather(reduce_weight.astype(jnp.bfloat16), "row", axis=0, tiled=True),
        lax.all_gather(reduce_bias.astype(jnp.bfloat16), "row", axis=1, tiled=True),
        lax.all_gather(first_gain.astype(jnp.bfloat16), "row", axis=1, tiled=True),
        lax.all_gather(first_shift.astype(jnp.bfloat16), "row", axis=1, tiled=True),
        lax.all_gather(second_gain.astype(jnp.bfloat16), "row", axis=1, tiled=True),
        lax.all_gather(second_shift.astype(jnp.bfloat16), "row", axis=1, tiled=True),
    )
    rows = to_rows(inputs).astype(jnp.float32)
    cotan_rows = to_rows(cotangent)
    tokens = rows.shape[0]
    width = rows.shape[1]
    clips = tokens // LEN
    local_heads = width // HD
    hidden_width = expand_mat.shape[1]
    gain_first = as_vector(gain_one)
    gain_second = as_vector(gain_two)
    normed_one, scaled_one, inverse_one = norm_shard(rows, gain_first, as_vector(shift_one))
    full_one = spread_rows(normed_one.astype(jnp.bfloat16))
    pairs = mixer_vec.astype(jnp.float32).reshape(local_heads, 2, HD)
    full_bias = jnp.stack([pairs[:, 0], jnp.zeros_like(pairs[:, 0]), pairs[:, 1]], axis=1).reshape(
        -1
    )
    mixed = (jnp.dot(full_one, mixer_mat, preferred_element_type=jnp.float32) + full_bias).astype(
        jnp.bfloat16
    )
    blocks = (
        mixed.reshape(clips, LEN, local_heads, 3, HD)
        .transpose(3, 0, 2, 1, 4)
        .reshape(3, clips * local_heads, LEN, HD)
    )
    head_blocks, logsums = lax.map(attend, (blocks[0], blocks[1], blocks[2]))
    heads = (
        head_blocks.reshape(clips, local_heads, LEN, HD)
        .transpose(0, 2, 1, 3)
        .reshape(tokens, width)
    )
    branch = lax.psum_scatter(
        jnp.dot(heads, merge_mat, preferred_element_type=jnp.float32),
        "col",
        scatter_dimension=1,
        tiled=True,
    )
    state = rows + branch + as_vector(merge_vec)
    normed_two, scaled_two, inverse_two = norm_shard(state, gain_second, as_vector(shift_two))
    full_two = spread_rows(normed_two.astype(jnp.bfloat16))
    hidden = jnp.dot(full_two, expand_mat, preferred_element_type=jnp.float32) + as_vector(
        expand_vec
    )
    active = exact_gelu(hidden).astype(jnp.bfloat16)
    down = lax.psum_scatter(
        jnp.dot(active, reduce_mat, preferred_element_type=jnp.float32).astype(jnp.bfloat16),
        "col",
        scatter_dimension=1,
        tiled=True,
    ).astype(jnp.float32)
    outputs = from_rows((state + down + as_vector(reduce_vec)).astype(jnp.bfloat16))
    cotan_full = gather_grads(cotan_rows)
    grad_reduce_mat = inner_rows(active, cotan_full)
    grad_reduce_vec = jnp.sum(cotan_rows.astype(jnp.float32), axis=0)
    grad_active = times_transposed(cotan_full, reduce_mat)
    gelu_pull = jax.vjp(exact_gelu, hidden)[1]
    grad_hidden = gelu_pull(grad_active)[0].astype(jnp.bfloat16)
    grad_expand_mat = inner_rows(full_two, grad_hidden)
    grad_expand_vec = jnp.sum(grad_hidden.astype(jnp.float32), axis=0)
    back_two, grad_gain_two, grad_shift_two = norm_back(
        times_transposed(grad_hidden, expand_mat), scaled_two, inverse_two, gain_second
    )
    grad_state = cotan_rows.astype(jnp.float32) + back_two
    grad_branch = grad_state.astype(jnp.bfloat16)
    branch_full = gather_grads(grad_branch)
    grad_merge_mat = inner_rows(heads, branch_full)
    grad_merge_vec = jnp.sum(grad_branch.astype(jnp.float32), axis=0)
    grad_heads = times_transposed(branch_full, merge_mat).astype(jnp.bfloat16)
    grad_blocks = (
        grad_heads.reshape(clips, LEN, local_heads, HD)
        .transpose(0, 2, 1, 3)
        .reshape(clips * local_heads, LEN, HD)
    )
    mixed_grads = lax.map(attend_back, (blocks[0], blocks[1], blocks[2], grad_blocks, logsums))
    grad_mixed = (
        mixed_grads.reshape(clips, local_heads, LEN, 3, HD)
        .transpose(0, 2, 1, 3, 4)
        .reshape(tokens, 3 * width)
    )
    grad_mixer_mat = inner_rows(full_one, grad_mixed)
    bias_sums = jnp.sum(grad_mixed.astype(jnp.float32), axis=0).reshape(local_heads, 3, HD)
    grad_mixer_vec = jnp.stack([bias_sums[:, 0], bias_sums[:, 2]], axis=1).reshape(
        local_heads, 2 * HD
    )
    back_one, grad_gain_one, grad_shift_one = norm_back(
        times_transposed(grad_mixed, mixer_mat), scaled_one, inverse_one, gain_first
    )
    input_grad = from_rows(grad_state + back_one)
    (
        part_mixer_mat,
        part_mixer_vec,
        part_merge_mat,
        part_merge_vec,
        part_expand_mat,
        part_expand_vec,
        part_reduce_mat,
        part_reduce_vec,
        part_gain_one,
        part_shift_one,
        part_gain_two,
        part_shift_two,
    ) = (
        lax.psum_scatter(grad_mixer_mat, "row", scatter_dimension=0, tiled=True),
        lax.psum_scatter(grad_mixer_vec, "row", scatter_dimension=1, tiled=True),
        lax.psum_scatter(grad_merge_mat, "row", scatter_dimension=0, tiled=True),
        lax.psum_scatter(
            grad_merge_vec.reshape(local_heads, HD), "row", scatter_dimension=1, tiled=True
        ),
        lax.psum_scatter(grad_expand_mat, "row", scatter_dimension=0, tiled=True),
        lax.psum_scatter(
            grad_expand_vec.reshape(local_heads, hidden_width // local_heads),
            "row",
            scatter_dimension=1,
            tiled=True,
        ),
        lax.psum_scatter(grad_reduce_mat, "row", scatter_dimension=0, tiled=True),
        lax.psum_scatter(
            grad_reduce_vec.reshape(local_heads, HD), "row", scatter_dimension=1, tiled=True
        ),
        lax.psum_scatter(
            grad_gain_one.reshape(local_heads, HD), "row", scatter_dimension=1, tiled=True
        ),
        lax.psum_scatter(
            grad_shift_one.reshape(local_heads, HD), "row", scatter_dimension=1, tiled=True
        ),
        lax.psum_scatter(
            grad_gain_two.reshape(local_heads, HD), "row", scatter_dimension=1, tiled=True
        ),
        lax.psum_scatter(
            grad_shift_two.reshape(local_heads, HD), "row", scatter_dimension=1, tiled=True
        ),
    )
    summed = lax.psum(
        (
            part_mixer_mat,
            part_mixer_vec,
            part_merge_mat,
            part_merge_vec,
            part_expand_mat,
            part_expand_vec,
            part_reduce_mat,
            part_reduce_vec,
            part_gain_one,
            part_shift_one,
            part_gain_two,
            part_shift_two,
        ),
        "dp",
    )
    return (
        outputs,
        input_grad,
        summed[0],
        summed[1],
        summed[2],
        summed[3],
        summed[4],
        summed[5],
        summed[6],
        summed[7],
        summed[8],
        summed[9],
        summed[10],
        summed[11],
    )


def solution(mesh):
    in_specs = (
        P(("dp", "row"), "col", None),
        P("row", "col"),
        P("col", "row"),
        P(("col", "row"), None),
        P("col", "row"),
        P("row", "col"),
        P("col", "row"),
        P(("col", "row"), None),
        P("col", "row"),
        P("col", "row"),
        P("col", "row"),
        P("col", "row"),
        P("col", "row"),
        P(("dp", "row"), "col", None),
    )
    out_specs = (
        P(("dp", "row"), "col", None),
        P(("dp", "row"), "col", None),
        P("row", "col"),
        P("col", "row"),
        P(("col", "row"), None),
        P("col", "row"),
        P("row", "col"),
        P("col", "row"),
        P(("col", "row"), None),
        P("col", "row"),
        P("col", "row"),
        P("col", "row"),
        P("col", "row"),
        P("col", "row"),
    )
    return jax.shard_map(body, mesh=mesh, in_specs=in_specs, out_specs=out_specs, check_vma=False)
```

profile of v0, /device:TPU:0, one launch (start us, length us, event | category | flops | bytes accessed | tf_op | source)
XLA Modules:
  0.0 1910.4 jit_solution(16474213476146647296)
XLA Ops:
  26.0 19.2 %psum.140 = f32[3642]{0:T(1024)S(1)} all-reduce(f32[3642]{0:T(1024)S(1)} %reduce_sum.167), channel_id=1, replica_groups=mesh['dp'=2,'row'=4,'col'=4] {'col'}, use_global_device_ids=true, to_apply=%region_1.0 | all-reduce | flops 3642 | bytes 29136 | tf_op jit(solution)/shard_map/psum | solution.py:49
  106.5 82.4 %all-gather.15.cloned.1.call-done = bf16[3642,768]{0,1:T(8,128)(2,1)} async-done(((bf16[3642,192]{0,1:T(8,128)(2,1)}), bf16[3642,768]{0,1:T(8,128)(2,1)}) %all-gather.15.cloned.1.call-update) | async-done | bytes 5594128 | tf_op jit(solution)/shard_map/all_gather | solution.py:62
  229.9 64.2 %while.22 = (s32[]{:T(128)}, bf16[9,1214,64]{1,2,0:T(8,128)(2,1)}, f32[9,1214]{1,0:T(8,128)}, bf16[9,1214,64]{2,1,0:T(8,128)(2,1)}, bf16[9,1214,64]{2,1,0:T(8,12...) while((s32[]{:T(128)}, bf16[9,1214,64]{1,2,0:T(8,128)(2,1)}, f32[9,1214]{1,0:T(8,128)}, ...), condition=%wide.region_7.8_spmd, body=%wide.region_4.7_spmd.sunk | while | flops 387684832 | bytes 18843696 | solution.py:174
  329.1 173.6 %reduce-scatter.33.cloned.1.call-done = f32[3642,192]{0,1:T(8,128)} async-done(((f32[3642,768]{0,1:T(8,128)}), f32[3642,192]{0,1:T(8,128)}) %reduce-scatter.33.cloned.1.call-update) | async-done | bytes 2797072 | tf_op jit(solution)/shard_map/reduce_scatter | solution.py:180
  505.7 18.5 psum.142
  569.6 76.5 %all-gather.17.cloned.1.call-done = bf16[3642,768]{0,1:T(8,128)(2,1)} async-done(((bf16[3642,192]{0,1:T(8,128)(2,1)}), bf16[3642,768]{0,1:T(8,128)(2,1)}) %all-gather.17.cloned.1.call-update) | async-done | bytes 5594128 | tf_op jit(solution)/shard_map/all_gather | solution.py:62
  663.7 107.1 %all-gather.23.cloned.1.call-done = bf16[3642,768]{0,1:T(8,128)(2,1)} async-done(((bf16[3642,192]{0,1:T(8,128)(2,1)}), bf16[3642,768]{0,1:T(8,128)(2,1)}) %all-gather.23.cloned.1.call-update) | async-done | bytes 5594128 | tf_op jit(solution)/shard_map/all_gather | solution.py:66
  770.8 35.6 %convert_reduce_fusion.1 = (f32[768]{0:T(1024)S(1)}, bf16[3642,768]{1,0:T(8,128)(2,1)S(1)}, f32[3642,768]{1,0:T(8,128)}) fusion(f32[3642,768]{1,0:T(8,128)} %fusion.63, f32[768]{0:T(1024)S(1)} %reshape.245, bf16[3642,768]{0,1:T(8,128)(2,1)} %all-gather.23.cloned.1.call-done, bf16[768,768]{1,0:T(8,128)(2,1)} %all-gather.21.cloned.1.call-done), kind=kOutput, calls=%fused_computation.57 | convolution fusion | flops 4506056704 | bytes 34750464 | tf_op jit(solution)/shard_map/dot_general | solution.py:39
  816.5 190.9 %reduce-scatter.37.cloned.1.call-done = f32[3642,192]{0,1:T(8,128)} async-done(((f32[3642,768]{0,1:T(8,128)}), f32[3642,192]{0,1:T(8,128)}) %reduce-scatter.37.cloned.1.call-update) | async-done | bytes 2797072 | tf_op jit(solution)/shard_map/reduce_scatter | solution.py:70
  1011.0 18.8 all-reduce.1
  1034.8 104.1 %all-gather.25.cloned.1.call-done = bf16[3642,768]{0,1:T(8,128)(2,1)} async-done(((bf16[3642,192]{0,1:T(8,128)(2,1)}), bf16[3642,768]{0,1:T(8,128)(2,1)}) %all-gather.25.cloned.1.call-update) | async-done | bytes 5594128 | tf_op jit(solution)/shard_map/all_gather | solution.py:66
  1150.2 102.2 %while.23 = (s32[]{:T(128)}, bf16[9,1214,3,64]{1,3,2,0:T(8,128)(2,1)}, bf16[9,1214,64]{2,1,0:T(8,128)(2,1)}, bf16[9,1214,64]{2,1,0:T(8,128)(2,1)}, f32[9,1214]{1...) while((s32[]{:T(128)}, ...), condition=%wide.region_21.22_spmd, body=%wide.region_19.21_spmd.sunk | while | flops 956805568 | bytes 48504736 | solution.py:222
  1355.5 118.8 %reduce-scatter.39.cloned.1.call-done = f32[3642,192]{0,1:T(8,128)} async-done(((f32[3642,768]{0,1:T(8,128)}), f32[3642,192]{0,1:T(8,128)}) %reduce-scatter.39.cloned.1.call-update) | async-done | bytes 2797072 | tf_op jit(solution)/shard_map/reduce_scatter | solution.py:70
  1498.6 21.8 %reduce-scatter.53.cloned.1.call-done = f32[64,3]{1,0:T(8,128)} async-done(((f32[256,3]{1,0:T(8,128)}), f32[64,3]{1,0:T(8,128)}) %reduce-scatter.53.cloned.1.call-update) | async-done | bytes 784
  1521.1 21.1 %reduce-scatter.63.cloned.1.call-done = f32[16,3]{1,0:T(8,128)} async-done(((f32[64,3]{1,0:T(8,128)}), f32[16,3]{1,0:T(8,128)}) %reduce-scatter.63.cloned.1.call-update) | async-done | bytes 208
  1543.0 21.2 %reduce-scatter.61.cloned.1.call-done = f32[16,3]{1,0:T(8,128)} async-done(((f32[64,3]{1,0:T(8,128)}), f32[16,3]{1,0:T(8,128)}) %reduce-scatter.61.cloned.1.call-update) | async-done | bytes 208
  1565.0 21.8 %reduce-scatter.51.cloned.1.call-done = f32[16,3]{1,0:T(8,128)} async-done(((f32[64,3]{1,0:T(8,128)}), f32[16,3]{1,0:T(8,128)}) %reduce-scatter.51.cloned.1.call-update) | async-done | bytes 208
  1587.5 21.6 %reduce-scatter.49.cloned.1.call-done = f32[32,3]{1,0:T(8,128)} async-done(((f32[128,3]{1,0:T(8,128)}), f32[32,3]{1,0:T(8,128)}) %reduce-scatter.49.cloned.1.call-update) | async-done | bytes 400
  1610.0 34.6 %reduce-scatter.47.cloned.1.call-done = f32[192,768]{1,0:T(8,128)} async-done(((f32[768,768]{1,0:T(8,128)}), f32[192,768]{1,0:T(8,128)}) %reduce-scatter.47.cloned.1.call-update) | async-done | bytes 589840 | tf_op jit(solution)/shard_map/reduce_scatter | solution.py:264
  1644.6 35.8 %reduce-scatter.45.cloned.1.call-done = f32[192,768]{1,0:T(8,128)} async-done(((f32[768,768]{1,0:T(8,128)}), f32[192,768]{1,0:T(8,128)}) %reduce-scatter.45.cloned.1.call-update) | async-done | bytes 589840 | tf_op jit(solution)/shard_map/reduce_scatter | solution.py:257
  1680.4 25.2 %reduce-scatter.43.cloned.1.call-done = f32[48,768]{1,0:T(8,128)} async-done(((f32[192,768]{1,0:T(8,128)}), f32[48,768]{1,0:T(8,128)}) %reduce-scatter.43.cloned.1.call-update) | async-done | bytes 147472 | tf_op jit(solution)/shard_map/reduce_scatter | solution.py:253
  1705.6 32.8 %reduce-scatter.41.cloned.1.call-done = f32[192,576]{1,0:T(8,128)} async-done(((f32[768,576]{1,0:T(8,128)}), f32[192,576]{1,0:T(8,128)}) %reduce-scatter.41.cloned.1.call-update) | async-done | bytes 442384 | tf_op jit(solution)/shard_map/reduce_scatter | solution.py:251
  1738.4 20.2 %all-reduce = (f32[3642]{0:T(1024)S(1)}, f32[3642]{0:T(1024)S(1)}) all-reduce(f32[3642]{0:T(1024)S(1)} %get-tuple-element.185, f32[3642]{0:T(1024)S(1)} %get-tuple-element.186), channel_id=1, replica_groups=mesh['dp'=2,'row'=4,'col'=4] {'col'}, use_global_device_ids=true, to_apply=%region_26.27 | all-reduce | flops 7284 | bytes 58272 | tf_op jit(solution)/shard_map/psum | solution.py:74
  1758.7 83.7 %reduce-scatter.35.cloned.1.call-done = bf16[3642,192]{0,1:T(8,128)(2,1)} async-done(((bf16[3642,768]{0,1:T(8,128)(2,1)}), bf16[3642,192]{0,1:T(8,128)(2,1)}) %reduce-scatter.35.cloned.1.call-update) | async-done | bytes 1398544 | tf_op jit(solution)/shard_map/reduce_scatter | solution.py:193
  (399 shorter events, 608.5 us)
Async XLA Ops:
  8.0 180.9 %all-gather.15.cloned.1.call-start = ((), (), s32[]{:S(2)}) async-start(), calls=%async_computation.16 | async-start | bytes 7127040 | tf_op jit(solution)/shard_map/all_gather | solution.py:62
  84.6 418.0 %reduce-scatter.33.cloned.1.call-start = ((), (), s32[]{:S(2)}) async-start(), calls=%async_computation.17 | async-start | bytes 14254080 | tf_op jit(solution)/shard_map/reduce_scatter | solution.py:180
  311.4 258.2 %all-gather.19.cloned.1.call-start = ((), (), s32[]{:S(2)}) async-start(), calls=%async_computation.19 | async-start | bytes 1474560 | tf_op jit(solution)/shard_map/all_gather | solution.py:142
  313.2 332.9 %all-gather.17.cloned.1.call-start = ((), (), s32[]{:S(2)}) async-start(), calls=%async_computation.18 | async-start | bytes 7127040 | tf_op jit(solution)/shard_map/all_gather | solution.py:62
  323.8 706.2 %copy-start.23 = (f32[192]{0:T(256)}, f32[192]{0:T(256)S(1)}, u32[]{:S(2)}) copy-start(f32[192]{0:T(256)S(1)} %reshape.243) | copy-start | bytes 2308
  541.8 121.9 %all-gather.21.cloned.1.call-start = ((), (), s32[]{:S(2)}) async-start(), calls=%async_computation.20 | async-start | bytes 1474560 | tf_op jit(solution)/shard_map/all_gather | solution.py:144
  543.7 227.1 %all-gather.23.cloned.1.call-start = ((), (), s32[]{:S(2)}) async-start(), calls=%async_computation.22 | async-start | bytes 7127040 | tf_op jit(solution)/shard_map/all_gather | solution.py:66
  564.3 443.1 %reduce-scatter.37.cloned.1.call-start = ((), (), s32[]{:S(2)}) async-start(), calls=%async_computation.23 | async-start | bytes 14254080 | tf_op jit(solution)/shard_map/reduce_scatter | solution.py:70
  816.3 322.6 %all-gather.25.cloned.1.call-start = ((), (), s32[]{:S(2)}) async-start(), calls=%async_computation.24 | async-start | bytes 7127040 | tf_op jit(solution)/shard_map/all_gather | solution.py:66
  1034.7 439.6 %reduce-scatter.39.cloned.1.call-start = ((), (), s32[]{:S(2)}) async-start(), calls=%async_computation.25 | async-start | bytes 14254080 | tf_op jit(solution)/shard_map/reduce_scatter | solution.py:70
  1283.0 214.8 %reduce-scatter.55.cloned.1.call-start = ((), (), s32[]{:S(2)}) async-start(), calls=%async_computation.33 | async-start | bytes 40960
  1285.4 234.9 %reduce-scatter.53.cloned.1.call-start = ((), (), s32[]{:S(2)}) async-start(), calls=%async_computation.32 | async-start | bytes 163840
  1286.3 256.0 %reduce-scatter.63.cloned.1.call-start = ((), (), s32[]{:S(2)}) async-start(), calls=%async_computation.37 | async-start | bytes 40960
  1287.2 277.1 %reduce-scatter.61.cloned.1.call-start = ((), (), s32[]{:S(2)}) async-start(), calls=%async_computation.36 | async-start | bytes 40960
  1288.0 298.7 %reduce-scatter.51.cloned.1.call-start = ((), (), s32[]{:S(2)}) async-start(), calls=%async_computation.31 | async-start | bytes 40960
  1300.0 309.2 %reduce-scatter.49.cloned.1.call-start = ((), (), s32[]{:S(2)}) async-start(), calls=%async_computation.30 | async-start | bytes 81920
  1309.1 335.5 %reduce-scatter.47.cloned.1.call-start = ((), (), s32[]{:S(2)}) async-start(), calls=%async_computation.29 | async-start | bytes 2949120 | tf_op jit(solution)/shard_map/reduce_scatter | solution.py:264
  1320.0 360.4 %reduce-scatter.45.cloned.1.call-start = ((), (), s32[]{:S(2)}) async-start(), calls=%async_computation.28 | async-start | bytes 2949120 | tf_op jit(solution)/shard_map/reduce_scatter | solution.py:257
  1330.6 375.0 %reduce-scatter.43.cloned.1.call-start = ((), (), s32[]{:S(2)}) async-start(), calls=%async_computation.27 | async-start | bytes 737280 | tf_op jit(solution)/shard_map/reduce_scatter | solution.py:253
  1335.9 402.5 %reduce-scatter.41.cloned.1.call-start = ((), (), s32[]{:S(2)}) async-start(), calls=%async_computation.26 | async-start | bytes 2457600 | tf_op jit(solution)/shard_map/reduce_scatter | solution.py:251
  1346.2 496.2 %reduce-scatter.35.cloned.1.call-start = ((), (), s32[]{:S(2)}) async-start(), calls=%async_computation.21 | async-start | bytes 7127040 | tf_op jit(solution)/shard_map/reduce_scatter | solution.py:193
  1355.5 525.1 %reduce-scatter.59.cloned.1.call-start = ((), (), s32[]{:S(2)}) async-start(), calls=%async_computation.35 | async-start | bytes 40960
  1479.6 406.7 %reduce-scatter.57.cloned.1.call-start = ((), (), s32[]{:S(2)}) async-start(), calls=%async_computation.34 | async-start | bytes 40960
  1485.6 410.2 %all-reduce.6.cloned.1.call-start = ((), (), s32[]{:S(2)}) async-start(), calls=%async_computation.38 | async-start | bytes 3637248 | tf_op jit(solution)/shard_map/psum | solution.py:281
  (35 other events, 5198.6 us)
Sparse Core Ops, SparseCore 0:
  84.8 104.1 all-gather.14
  311.5 191.0 reduce-scatter.32
  1034.8 104.0 all-gather.24
  1283.1 191.1 reduce-scatter.38
  1477.1 20.6 reduce-scatter.54
  1500.6 19.6 reduce-scatter.52
  1522.7 19.5 reduce-scatter.62
  1544.7 19.5 reduce-scatter.60
  1567.2 19.5 reduce-scatter.50
  1589.6 19.5 reduce-scatter.48
  1611.7 32.8 reduce-scatter.46
  1647.5 32.8 reduce-scatter.44
  1683.5 22.0 reduce-scatter.42
  1708.0 30.3 reduce-scatter.40
  1740.6 101.7 reduce-scatter.34
  1844.6 19.8 reduce-scatter.58
  1866.7 19.5 reduce-scatter.56
Sparse Core Ops, SparseCore 1:
  314.0 15.6 all-gather.18
  541.9 104.1 all-gather.16
  648.1 15.5 all-gather.20
  665.3 105.4 all-gather.22
  816.4 191.0 reduce-scatter.36
  1738.5 56.7 all-reduce.5
where the time goes:
time: 1920 us; the launch traced here: 1910 us
  waiting for transfers between devices  1200 us (62%)
  matrix products  251 us (13%)
  local copies, waits for them, and re-layouts  193 us (10%)
  blocking collectives  175 us (9%)
  other arithmetic  76.7 us (4%)
    reduce_scatter x2, waiting for transfers between devices, norm_back(): lax.psum_scatter(partial_rows, 'col', scatter_dimension=1, tiled=True)  310 us
    all_gather x2, waiting for transfers between devices, gather_grads(): return lax.all_gather(values, 'col', axis=1, tiled=True)  211 us
    reduce_scatter x1, waiting for transfers between devices, body(): lax.psum_scatter(jnp.dot(heads, merge_mat, preferred_element_type=jnp.flo...  174 us
    all_gather x2, waiting for transfers between devices, spread_rows(): return lax.all_gather(values, 'col', axis=1, tiled=True)  159 us
    unnamed x31, waiting for transfers between devices  125 us
    dot_general x31, matrix products, times_transposed(): lax.dot_general(left, right, (((1,), (1,)), ((), ())), preferred_element_...  111 us
    reduce_scatter x1, waiting for transfers between devices, body(): lax.psum_scatter(jnp.dot(active, reduce_mat, preferred_element_type=jnp.f...  83.7 us
    psum x4, blocking collectives, row_sum(): return lax.psum(values, 'col')  68.8 us
  transfers between devices with their start and end apart: 23, of which 20 were waited for; matrix products, arithmetic and copies ran while one was open for 8% of the time, Pallas kernels for 0%

commit v1 on v0

--- a/solution.py
+++ b/solution.py
@@ -7,6 +7,18 @@
 HD = 64
 LEN = 1214
 EPSILON = 1e-06
+
+
+def collect(shard, axis, dim):
+    ways, here = (lax.axis_size(axis), lax.axis_index(axis))
+    grown, reach = (shard, 1)
+    while reach < ways:
+        theirs = lax.ppermute(grown, axis, [(d, d ^ reach) for d in range(ways)])
+        mine_first = jnp.concatenate([grown, theirs], axis=dim)
+        theirs_first = jnp.concatenate([theirs, grown], axis=dim)
+        grown = jnp.where(here & reach == 0, mine_first, theirs_first)
+        reach = 2 * reach
+    return grown
 
 
 def to_rows(values):
@@ -63,7 +75,7 @@
 
 
 def gather_grads(values):
-    return lax.all_gather(values, "col", axis=1, tiled=True)
+    return collect(values, "col", 1)
 
 
 def norm_back(partial_rows, scaled, inverse, gain):

time: 1920 us -> 2030 us (1.057)
  waiting for transfers between devices: 1200 us -> 1270 us
  local copies, waits for them, and re-layouts: 193 us -> 221 us
    ppermute x0 -> x4, waiting for transfers between devices: none -> 366 us  [collect(): theirs = lax.ppermute(grown, axis, [(d, d ^ reach) for d in range(ways)])]
    all_gather x2 -> x0, waiting for transfers between devices: 211 us -> none  [gather_grads(): return lax.all_gather(values, 'col', axis=1, tiled=True)]
    all_gather x2, waiting for transfers between devices: 159 us -> 82.4 us  [spread_rows(): return lax.all_gather(values, 'col', axis=1, tiled=True)]
    unnamed x31 -> x29, waiting for transfers between devices: 125 us -> 125 us
  transfers between devices with their start and end apart: 23 -> 25, of which waited for: 20 -> 20; matrix products, arithmetic and copies ran while one was open for 8% -> 9% of each run, Pallas kernels for 0% -> 0%
where the time goes in v1:
time: 2030 us; the launch traced here: 2020 us
  waiting for transfers between devices  1270 us (63%)
  matrix products  255 us (13%)
  local copies, waits for them, and re-layouts  221 us (11%)
  blocking collectives  175 us (9%)
  other arithmetic  81 us (4%)
    ppermute x4, waiting for transfers between devices, collect(): theirs = lax.ppermute(grown, axis, [(d, d ^ reach) for d in range(ways)])  366 us
    reduce_scatter x2, waiting for transfers between devices, norm_back(): lax.psum_scatter(partial_rows, 'col', scatter_dimension=1, tiled=True)  309 us
    reduce_scatter x1, waiting for transfers between devices, body(): lax.psum_scatter(jnp.dot(heads, merge_mat, preferred_element_type=jnp.flo...  174 us
    unnamed x29, waiting for transfers between devices  125 us
    dot_general x31, matrix products, times_transposed(): lax.dot_general(left, right, (((1,), (1,)), ((), ())), preferred_element_...  114 us
    reduce_scatter x1, waiting for transfers between devices, body(): lax.psum_scatter(jnp.dot(active, reduce_mat, preferred_element_type=jnp.f...  83.9 us
    all_gather x2, waiting for transfers between devices, spread_rows(): return lax.all_gather(values, 'col', axis=1, tiled=True)  82.4 us
    psum x4, blocking collectives, row_sum(): return lax.psum(values, 'col')  68.8 us
  transfers between devices with their start and end apart: 25, of which 20 were waited for; matrix products, arithmetic and copies ran while one was open for 9% of the time, Pallas kernels for 0%

profile of v1, /device:TPU:0, one launch (start us, length us, event | category | flops | bytes accessed | tf_op | source)
XLA Modules:
  0.0 2019.8 jit_solution(11491754327013492149)
XLA Ops:
  26.0 19.2 psum.140
  106.5 82.4 %all-gather.13.cloned.1.call-done = bf16[3642,768]{0,1:T(8,128)(2,1)} async-done(((bf16[3642,192]{0,1:T(8,128)(2,1)}), bf16[3642,768]{0,1:T(8,128)(2,1)}) %all-gather.13.cloned.1.call-update) | async-done | bytes 5594128 | tf_op jit(solution)/shard_map/all_gather | solution.py:74
  230.0 64.2 %while.22 = (s32[]{:T(128)}, bf16[9,1214,64]{1,2,0:T(8,128)(2,1)}, f32[9,1214]{1,0:T(8,128)}, bf16[9,1214,64]{2,1,0:T(8,128)(2,1)}, bf16[9,1214,64]{2,1,0:T(8,12...) while((s32[]{:T(128)}, bf16[9,1214,64]{1,2,0:T(8,128)(2,1)}, f32[9,1214]{1,0:T(8,128)}, ...), condition=%wide.region_7.8_spmd, body=%wide.region_4.7_spmd.sunk | while | flops 387684832 | bytes 18843696 | solution.py:186
  329.3 173.6 %reduce-scatter.33.cloned.1.call-done = f32[3642,192]{0,1:T(8,128)} async-done(((f32[3642,768]{0,1:T(8,128)}), f32[3642,192]{0,1:T(8,128)}) %reduce-scatter.33.cloned.1.call-update) | async-done | bytes 2797072 | tf_op jit(solution)/shard_map/reduce_scatter | solution.py:192
  562.3 103.1 %collective-permute-done = bf16[3642,192]{0,1:T(8,128)(2,1)} collective-permute-done((bf16[3642,192]{0,1:T(8,128)(2,1)}, bf16[3642,192]{0,1:T(8,128)(2,1)}, u32[]{:S(2)}, u32[]{:S(2)}) %collective-permute-start) | collective-permute-done | bytes 1398560 | tf_op jit(solution)/shard_map/ppermute | solution.py:16
  681.4 115.1 %collective-permute-done.1 = bf16[3642,384]{1,0:T(8,128)(2,1)} collective-permute-done((bf16[3642,384]{1,0:T(8,128)(2,1)}, bf16[3642,384]{1,0:T(8,128)(2,1)}, u32[]{:S(2)}, u32[]{:S(2)}) %collective-permute-start.1) | collective-permute-done | bytes 2797088 | tf_op jit(solution)/shard_map/ppermute | solution.py:16
  821.5 36.7 %convert_reduce_fusion.1 = (f32[768]{0:T(1024)S(1)}, bf16[3642,768]{1,0:T(8,128)(2,1)S(1)}, f32[3642,768]{1,0:T(8,128)}) fusion(f32[3642,768]{1,0:T(8,128)} %fusion.70, f32[768]{0:T(1024)S(1)} %reshape.245, bf16[768,768]{1,0:T(8,128)(2,1)} %all-gather.19.cloned.1.call-done, bf16[3642,384]{0,1:T(8,128)(2,1)} %copy.178, ...), kind=kOutput, calls=%fused_computation.57 | convolution fusion | flops 4531229696 | bytes 34750464 | tf_op jit(solution)/shard_map/dot_general | solution.py:51
  868.2 191.1 %reduce-scatter.37.cloned.1.call-done = f32[3642,192]{0,1:T(8,128)} async-done(((f32[3642,768]{0,1:T(8,128)}), f32[3642,192]{0,1:T(8,128)}) %reduce-scatter.37.cloned.1.call-update) | async-done | bytes 2797072 | tf_op jit(solution)/shard_map/reduce_scatter | solution.py:82
  1063.0 19.1 all-reduce.1
  1085.9 29.3 %collective-permute-done.2 = bf16[3642,192]{0,1:T(8,128)(2,1)S(1)} collective-permute-done((bf16[3642,192]{0,1:T(8,128)(2,1)S(1)}, bf16[3642,192]{0,1:T(8,128)(2,1)S(1)}, u32[]{:S(2)}, u32[]{:S(2)}) %collective-permute-start.2) | collective-permute-done | bytes 1398560 | tf_op jit(solution)/shard_map/ppermute | solution.py:16
  1120.2 118.6 %collective-permute-done.3 = bf16[3642,384]{1,0:T(8,128)(2,1)} collective-permute-done((bf16[3642,384]{1,0:T(8,128)(2,1)}, bf16[3642,384]{1,0:T(8,128)(2,1)}, u32[]{:S(2)}, u32[]{:S(2)}) %collective-permute-start.3) | collective-permute-done | bytes 2797088 | tf_op jit(solution)/shard_map/ppermute | solution.py:16
  1259.2 102.6 %while.23 = (s32[]{:T(128)}, bf16[9,1214,3,64]{1,3,2,0:T(8,128)(2,1)}, bf16[9,1214,64]{2,1,0:T(8,128)(2,1)}, bf16[9,1214,64]{2,1,0:T(8,128)(2,1)}, f32[9,1214]{1...) while((s32[]{:T(128)}, ...), condition=%wide.region_21.22_spmd, body=%wide.region_19.21_spmd.sunk | while | flops 956805568 | bytes 48504736 | solution.py:234
  1465.2 117.9 %reduce-scatter.39.cloned.1.call-done = f32[3642,192]{0,1:T(8,128)} async-done(((f32[3642,768]{0,1:T(8,128)}), f32[3642,192]{0,1:T(8,128)}) %reduce-scatter.39.cloned.1.call-update) | async-done | bytes 2797072 | tf_op jit(solution)/shard_map/reduce_scatter | solution.py:82
  1607.3 21.7 %reduce-scatter.53.cloned.1.call-done = f32[64,3]{1,0:T(8,128)} async-done(((f32[256,3]{1,0:T(8,128)}), f32[64,3]{1,0:T(8,128)}) %reduce-scatter.53.cloned.1.call-update) | async-done | bytes 784
  1629.9 21.0 %reduce-scatter.63.cloned.1.call-done = f32[16,3]{1,0:T(8,128)} async-done(((f32[64,3]{1,0:T(8,128)}), f32[16,3]{1,0:T(8,128)}) %reduce-scatter.63.cloned.1.call-update) | async-done | bytes 208
  1651.7 21.2 %reduce-scatter.61.cloned.1.call-done = f32[16,3]{1,0:T(8,128)} async-done(((f32[64,3]{1,0:T(8,128)}), f32[16,3]{1,0:T(8,128)}) %reduce-scatter.61.cloned.1.call-update) | async-done | bytes 208
  1673.7 21.8 %reduce-scatter.51.cloned.1.call-done = f32[16,3]{1,0:T(8,128)} async-done(((f32[64,3]{1,0:T(8,128)}), f32[16,3]{1,0:T(8,128)}) %reduce-scatter.51.cloned.1.call-update) | async-done | bytes 208
  1696.2 21.9 %reduce-scatter.49.cloned.1.call-done = f32[32,3]{1,0:T(8,128)} async-done(((f32[128,3]{1,0:T(8,128)}), f32[32,3]{1,0:T(8,128)}) %reduce-scatter.49.cloned.1.call-update) | async-done | bytes 400
  1718.8 34.4 %reduce-scatter.47.cloned.1.call-done = f32[192,768]{1,0:T(8,128)} async-done(((f32[768,768]{1,0:T(8,128)}), f32[192,768]{1,0:T(8,128)}) %reduce-scatter.47.cloned.1.call-update) | async-done | bytes 589840 | tf_op jit(solution)/shard_map/reduce_scatter | solution.py:276
  1753.3 36.0 %reduce-scatter.45.cloned.1.call-done = f32[192,768]{1,0:T(8,128)} async-done(((f32[768,768]{1,0:T(8,128)}), f32[192,768]{1,0:T(8,128)}) %reduce-scatter.45.cloned.1.call-update) | async-done | bytes 589840 | tf_op jit(solution)/shard_map/reduce_scatter | solution.py:269
  1789.2 25.1 %reduce-scatter.43.cloned.1.call-done = f32[48,768]{1,0:T(8,128)} async-done(((f32[192,768]{1,0:T(8,128)}), f32[48,768]{1,0:T(8,128)}) %reduce-scatter.43.cloned.1.call-update) | async-done | bytes 147472 | tf_op jit(solution)/shard_map/reduce_scatter | solution.py:265
  1814.3 32.9 %reduce-scatter.41.cloned.1.call-done = f32[192,576]{1,0:T(8,128)} async-done(((f32[768,576]{1,0:T(8,128)}), f32[192,576]{1,0:T(8,128)}) %reduce-scatter.41.cloned.1.call-update) | async-done | bytes 442384 | tf_op jit(solution)/shard_map/reduce_scatter | solution.py:263
  1847.2 20.0 all-reduce
  1867.2 83.9 %reduce-scatter.35.cloned.1.call-done = bf16[3642,192]{0,1:T(8,128)(2,1)} async-done(((bf16[3642,768]{0,1:T(8,128)(2,1)}), bf16[3642,192]{0,1:T(8,128)(2,1)}) %reduce-scatter.35.cloned.1.call-update) | async-done | bytes 1398544 | tf_op jit(solution)/shard_map/reduce_scatter | solution.py:205
  (411 shorter events, 656.1 us)
Async XLA Ops:
  8.0 180.9 %all-gather.13.cloned.1.call-start = ((), (), s32[]{:S(2)}) async-start(), calls=%async_computation.16 | async-start | bytes 7127040 | tf_op jit(solution)/shard_map/all_gather | solution.py:74
  84.6 418.2 %reduce-scatter.33.cloned.1.call-start = ((), (), s32[]{:S(2)}) async-start(), calls=%async_computation.17 | async-start | bytes 14254080 | tf_op jit(solution)/shard_map/reduce_scatter | solution.py:192
  311.6 498.3 %all-gather.17.cloned.1.call-start = ((), (), s32[]{:S(2)}) async-start(), calls=%async_computation.19 | async-start | bytes 1474560 | tf_op jit(solution)/shard_map/all_gather | solution.py:154
  313.4 496.6 %all-gather.15.cloned.1.call-start = ((), (), s32[]{:S(2)}) async-start(), calls=%async_computation.18 | async-start | bytes 7127040 | tf_op jit(solution)/shard_map/all_gather | solution.py:74
  542.0 279.6 %all-gather.19.cloned.1.call-start = ((), (), s32[]{:S(2)}) async-start(), calls=%async_computation.20 | async-start | bytes 1474560 | tf_op jit(solution)/shard_map/all_gather | solution.py:156
  562.2 103.2 %collective-permute-start = (bf16[3642,192]{0,1:T(8,128)(2,1)}, bf16[3642,192]{0,1:T(8,128)(2,1)}, u32[]{:S(2)}, u32[]{:S(2)}) collective-permute-start(bf16[3642,192]{0,1:T(8,128)(2,1)} %copy.173), channel_id=1, source_target_pairs={{0,1},{1,0},{2,3},{3,2},{4,5},{5,4},{6,7},{7,6},{8,9},{9,8},{10,11... | collective-permute-start | bytes 4195592 | tf_op jit(solution)/shard_map/ppermute | solution.py:16
  674.3 122.2 %collective-permute-start.1 = (bf16[3642,384]{1,0:T(8,128)(2,1)}, bf16[3642,384]{1,0:T(8,128)(2,1)}, u32[]{:S(2)}, u32[]{:S(2)}) collective-permute-start(bf16[3642,384]{1,0:T(8,128)(2,1)} %copy.177), channel_id=1, source_target_pairs={{0,2},{1,3},{2,0},{3,1},{4,6},{5,7},{6,4},{7,5},{8,10},{9,11},{10,... | collective-permute-start | bytes 8391176 | tf_op jit(solution)/shard_map/ppermute | solution.py:16
  676.1 383.3 %reduce-scatter.37.cloned.1.call-start = ((), (), s32[]{:S(2)}) async-start(), calls=%async_computation.22 | async-start | bytes 14254080 | tf_op jit(solution)/shard_map/reduce_scatter | solution.py:82
  868.2 714.9 %reduce-scatter.39.cloned.1.call-start = ((), (), s32[]{:S(2)}) async-start(), calls=%async_computation.23 | async-start | bytes 14254080 | tf_op jit(solution)/shard_map/reduce_scatter | solution.py:82
  1119.6 119.2 %collective-permute-start.3 = (bf16[3642,384]{1,0:T(8,128)(2,1)}, bf16[3642,384]{1,0:T(8,128)(2,1)}, u32[]{:S(2)}, u32[]{:S(2)}) collective-permute-start(bf16[3642,384]{1,0:T(8,128)(2,1)} %copy.180), channel_id=1, source_target_pairs={{0,2},{1,3},{2,0},{3,1},{4,6},{5,7},{6,4},{7,5},{8,10},{9,11},{10,... | collective-permute-start | bytes 8391176 | tf_op jit(solution)/shard_map/ppermute | solution.py:16
  1392.3 214.3 %reduce-scatter.55.cloned.1.call-start = ((), (), s32[]{:S(2)}) async-start(), calls=%async_computation.31 | async-start | bytes 40960
  1394.6 234.4 %reduce-scatter.53.cloned.1.call-start = ((), (), s32[]{:S(2)}) async-start(), calls=%async_computation.30 | async-start | bytes 163840
  1395.5 255.4 %reduce-scatter.63.cloned.1.call-start = ((), (), s32[]{:S(2)}) async-start(), calls=%async_computation.35 | async-start | bytes 40960
  1396.4 276.5 %reduce-scatter.61.cloned.1.call-start = ((), (), s32[]{:S(2)}) async-start(), calls=%async_computation.34 | async-start | bytes 40960
  1397.3 298.2 %reduce-scatter.51.cloned.1.call-start = ((), (), s32[]{:S(2)}) async-start(), calls=%async_computation.29 | async-start | bytes 40960
  1409.0 309.0 %reduce-scatter.49.cloned.1.call-start = ((), (), s32[]{:S(2)}) async-start(), calls=%async_computation.28 | async-start | bytes 81920
  1418.2 335.0 %reduce-scatter.47.cloned.1.call-start = ((), (), s32[]{:S(2)}) async-start(), calls=%async_computation.27 | async-start | bytes 2949120 | tf_op jit(solution)/shard_map/reduce_scatter | solution.py:276
  1428.9 360.3 %reduce-scatter.45.cloned.1.call-start = ((), (), s32[]{:S(2)}) async-start(), calls=%async_computation.26 | async-start | bytes 2949120 | tf_op jit(solution)/shard_map/reduce_scatter | solution.py:269
  1439.7 374.5 %reduce-scatter.43.cloned.1.call-start = ((), (), s32[]{:S(2)}) async-start(), calls=%async_computation.25 | async-start | bytes 737280 | tf_op jit(solution)/shard_map/reduce_scatter | solution.py:265
  1445.6 401.7 %reduce-scatter.41.cloned.1.call-start = ((), (), s32[]{:S(2)}) async-start(), calls=%async_computation.24 | async-start | bytes 2457600 | tf_op jit(solution)/shard_map/reduce_scatter | solution.py:263
  1455.6 495.6 %reduce-scatter.35.cloned.1.call-start = ((), (), s32[]{:S(2)}) async-start(), calls=%async_computation.21 | async-start | bytes 7127040 | tf_op jit(solution)/shard_map/reduce_scatter | solution.py:205
  1464.9 524.5 %reduce-scatter.59.cloned.1.call-start = ((), (), s32[]{:S(2)}) async-start(), calls=%async_computation.33 | async-start | bytes 40960
  1588.4 406.9 %reduce-scatter.57.cloned.1.call-start = ((), (), s32[]{:S(2)}) async-start(), calls=%async_computation.32 | async-start | bytes 40960
  1594.3 410.4 %all-reduce.6.cloned.1.call-start = ((), (), s32[]{:S(2)}) async-start(), calls=%async_computation.36 | async-start | bytes 3637248 | tf_op jit(solution)/shard_map/psum | solution.py:293
  (39 other events, 6365.9 us)
Sparse Core Ops, SparseCore 0:
  84.8 104.1 all-gather.12
  311.7 191.0 reduce-scatter.32
  1392.4 190.6 reduce-scatter.38
  1585.9 20.5 reduce-scatter.54
  1609.4 19.6 reduce-scatter.52
  1631.3 19.5 reduce-scatter.62
  1653.3 19.5 reduce-scatter.60
  1675.9 19.5 reduce-scatter.50
  1698.4 19.5 reduce-scatter.48
  1720.4 32.7 reduce-scatter.46
  1756.4 32.8 reduce-scatter.44
  1792.1 22.0 reduce-scatter.42
  1816.8 30.3 reduce-scatter.40
  1849.4 101.7 reduce-scatter.34
  1953.4 19.9 reduce-scatter.58
  1975.7 19.5 reduce-scatter.56
Sparse Core Ops, SparseCore 1:
  314.2 15.6 all-gather.16
  542.1 132.5 all-gather.14
  676.6 17.9 all-gather.18
  868.3 191.1 reduce-scatter.36
  1847.3 56.7 all-reduce.5
